TPU v7x, 256 devices: a whole 4x4x8 slice. The times are simulated.
256 devices in a mesh: seq: 32 (over z, x), win: 4 (over y), wout: 2 (over core).
Axes of the slice: x: 4, y: 4, z: 8, core: 2. Of those that a mesh axis runs over, the one named last changes fastest.
Arguments:
- qkv_in: bfloat16 [8192, 3, 2048], P('seq', None, ('win', 'wout')), may hold values from -6 to 6
- conv_w: float32 [3, 4, 2048], P(None, None, ('win', 'wout')), may hold values from -3 to 3
- beta_logits: float32 [16, 8192], P(('win', 'wout'), 'seq'), may hold values from -10 to 3
- lengths: int32 [4], replicated, may hold values from 1 to 3968, as said below
- out_gain: float32 [128], replicated, may hold values from 0.1 to 1.9
- w_out: bfloat16 [2048, 2048], P(('win', 'wout')), may hold values from -0.125 to 0.125
- hidden_in: bfloat16 [8192, 2048], P(('seq', 'win', 'wout')), may hold values from -6 to 6
- norm_gain: float32 [2048], replicated, may hold values from 0.1 to 1.9
- w_qkv: bfloat16 [2048, 6144], P('win', 'wout'), may hold values from -0.125 to 0.125
Outputs:
- qkv_next: bfloat16 [8192, 6144], P(('seq', 'win'), 'wout')
- stream_out: bfloat16 [8192, 2048], P(('seq', 'win', 'wout'))
- final_states: float32 [4, 16, 128, 128], P(None, ('win', 'wout'))
- conv_edges: bfloat16 [4, 3, 3, 2048], P(None, None, None, ('win', 'wout'))
Inputs may be any that keep to these rules, and one draw needn't show every extreme that they name: The lengths sum to 8192; the largest is exactly 3968.
All inputs are finite; a program needn't handle non-finite values.
Results may differ from a plain program's by a relative error of at most 0.022.
Values may be sent and summed in bfloat16 or wider, within the bound.
No kernel may reach another device: no remote copies, remote signals or barrier semaphores. Data moves between devices by JAX's collectives and lax.ppermute only.
A program may use at most 64 MiB of HBM per device.

v0:
```python
import jax
import jax.numpy as jnp
from jax import lax
from jax.sharding import PartitionSpec as P

DK = 128
CONV = 4
SPAN = 64
REQS = 4


def from_behind(value, axis, steps):
    count = lax.axis_size(axis)
    leading, last = (max(0, -steps), min(count, count - steps))
    return lax.ppermute(value, axis, [(source, source + steps) for source in range(leading, last)])


def segment_ids(positions, seg_ends):
    counts = jnp.sum((positions[:, None] >= seg_ends[None, :]).astype(jnp.int32), axis=1)
    return jnp.where(positions < 0, -1, counts)


def unit_rows(values):
    return values / jnp.sqrt(jnp.sum(values * values, axis=-1, keepdims=True) + 1e-06)


def outer_product(form, left, right):
    return jnp.einsum(form, left, right, precision=lax.Precision.HIGHEST)


def body(qkv_in, conv_w, beta_logits, lengths, out_gain, w_out, hidden_in, norm_gain, w_qkv):
    row_count = qkv_in.shape[0]
    local_width = qkv_in.shape[2]
    head_count = local_width // DK
    rim_rows = CONV - 1
    first_position = lax.axis_index("seq") * row_count
    seg_ends = jnp.cumsum(lengths)
    preceding_entries = from_behind(qkv_in[row_count - rim_rows :], "seq", 1)
    extended = jnp.concatenate([preceding_entries, qkv_in], axis=0)
    ext_pos = first_position - rim_rows + jnp.arange(row_count + rim_rows, dtype=jnp.int32)
    ext_seg = segment_ids(ext_pos, seg_ends)
    own_seg = ext_seg[rim_rows:]
    pre = jnp.zeros((row_count, 3, local_width), jnp.float32)
    for offset in range(CONV):
        same_request = (ext_seg[offset : offset + row_count] == own_seg).astype(jnp.float32)
        window = extended[offset : offset + row_count].astype(jnp.float32)
        pre = pre + conv_w[:, offset, :][None] * window * same_request[:, None, None]
    activated = jax.nn.silu(pre).astype(jnp.bfloat16)
    span_count = row_count // SPAN

    def blocks(values):
        return values.reshape(span_count, SPAN, head_count, DK).transpose(0, 2, 1, 3)

    query = blocks(
        unit_rows(activated[:, 0].astype(jnp.float32).reshape(row_count, head_count, DK))
    )
    keys_b = blocks(
        unit_rows(activated[:, 1].astype(jnp.float32).reshape(row_count, head_count, DK))
    )
    values_b = blocks(activated[:, 2].astype(jnp.float32).reshape(row_count, head_count, DK))
    beta_coefficient = (
        jax.nn.sigmoid(beta_logits).reshape(head_count, span_count, SPAN).transpose(1, 0, 2)
    )
    seg_blocks = own_seg.reshape(span_count, SPAN)
    before_seg = segment_ids(
        first_position + jnp.arange(span_count, dtype=jnp.int32) * SPAN - 1, seg_ends
    )
    coupled_entries = (seg_blocks == before_seg[:, None]).astype(jnp.float32)
    same = seg_blocks[:, :, None] == seg_blocks[:, None, :]
    row_ids = jnp.arange(SPAN)[:, None]
    col_ids = jnp.arange(SPAN)[None, :]
    strict = (same & (row_ids > col_ids)).astype(jnp.float32)
    causal = (same & (row_ids >= col_ids)).astype(jnp.float32)
    gram = outer_product("nhik,nhjk->nhij", keys_b, keys_b)
    system = (
        jnp.eye(SPAN, dtype=jnp.float32) + beta_coefficient[..., :, None] * gram * strict[:, None]
    )
    targets = jnp.concatenate(
        [
            beta_coefficient[..., None] * values_b,
            (beta_coefficient * coupled_entries[:, None])[..., None] * keys_b,
        ],
        axis=-1,
    )
    solved = lax.linalg.triangular_solve(
        system, targets, left_side=True, lower=True, unit_diagonal=True
    )
    u_local = solved[..., :DK]
    w_link = solved[..., DK:]
    scores = outer_product("nhik,nhjk->nhij", query, keys_b) * causal[:, None]
    out_local = outer_product("nhij,nhjv->nhiv", scores, u_local)
    query_link = coupled_entries[:, None, :, None] * query - outer_product(
        "nhij,nhjk->nhik", scores, w_link
    )
    eye_keys = jnp.eye(DK, dtype=jnp.float32)
    last_link = coupled_entries[:, -1]
    in_last = (seg_blocks == seg_blocks[:, -1:]).astype(jnp.float32)
    trans = last_link[:, None, None, None] * (
        eye_keys - outer_product("nhjk,nhjl->nhkl", keys_b, w_link)
    )
    write = outer_product("nhjk,nhjv->nhkv", keys_b * in_last[:, None, :, None], u_local)

    def fold_span(carried_state, state_pair):
        return (
            (
                outer_product("hkl,hlm->hkm", state_pair[0], carried_state[0]),
                outer_product("eat,eto->eao", state_pair[0], carried_state[1]) + state_pair[1],
            ),
            None,
        )

    identity_maps = (
        jnp.broadcast_to(eye_keys, (head_count, DK, DK)),
        jnp.zeros((head_count, DK, DK), jnp.float32),
    )
    (device_transition, device_update), unused = lax.scan(fold_span, identity_maps, (trans, write))

    def chain_step(hop_index, incoming_state):
        outgoing_state = (
            outer_product("eat,eto->eao", device_transition, incoming_state) + device_update
        )
        return from_behind(outgoing_state, "seq", 1)

    state_in = lax.fori_loop(0, lax.axis_size("seq") - 1, chain_step, jnp.zeros_like(device_update))

    def advance(memory_state, state_pair):
        return (
            outer_product("eat,eto->eao", state_pair[0], memory_state) + state_pair[1],
            memory_state,
        )

    unused_end, entry_states = lax.scan(advance, state_in, (trans, write))
    attended = out_local + outer_product("nhik,nhkv->nhiv", query_link, entry_states)
    corrected_values = u_local - outer_product("nhik,nhkv->nhiv", w_link, entry_states)
    positions = (first_position + jnp.arange(row_count, dtype=jnp.int32)).reshape(span_count, SPAN)
    last_tok = seg_ends - 1
    at_end = (positions[None] == last_tok[:, None, None]).astype(jnp.float32)
    ends_here = jnp.sum(at_end, axis=2)
    request_ids = jnp.arange(REQS, dtype=jnp.int32)
    member = (seg_blocks[None] == request_ids[:, None, None]).astype(jnp.float32) * ends_here[
        ..., None
    ]
    carried = jnp.sum(at_end * coupled_entries[None], axis=2)
    req_states = outer_product("rn,nhkv->rhkv", carried, entry_states)
    req_states = req_states + jnp.einsum(
        "rnj,nhjk,nhjv->rhkv", member, keys_b, corrected_values, precision=lax.Precision.HIGHEST
    )
    owned = (last_tok >= first_position) & (last_tok < first_position + row_count)
    wanted = last_tok[:, None] - rim_rows + 1 + jnp.arange(rim_rows, dtype=jnp.int32)[None, :]
    select = (
        (ext_pos[None, None, :] == wanted[:, :, None])
        & (ext_seg[None, None, :] == request_ids[:, None, None])
        & owned[:, None, None]
    )
    edge_vals = jnp.einsum(
        "rim,mcj->ricj", select.astype(jnp.bfloat16), extended, preferred_element_type=jnp.float32
    )
    totals = (
        lax.psum(req_states.astype(jnp.bfloat16), "seq").astype(jnp.float32),
        lax.psum(edge_vals.astype(jnp.bfloat16), "seq").astype(jnp.float32),
    )
    final_states = totals[0]
    conv_edges = totals[1].astype(jnp.bfloat16)
    heads_rows = attended.transpose(0, 2, 1, 3).reshape(row_count, head_count, DK)
    scale_heads = jnp.sqrt(jnp.mean(heads_rows * heads_rows, axis=-1, keepdims=True) + 1e-05)
    normed_heads = (
        (heads_rows / scale_heads * out_gain).reshape(row_count, local_width).astype(jnp.bfloat16)
    )
    mixed = lax.psum_scatter(
        jnp.dot(normed_heads, w_out, preferred_element_type=jnp.float32).astype(jnp.bfloat16),
        ("win", "wout"),
        scatter_dimension=0,
        tiled=True,
    ).astype(jnp.float32)
    summed = hidden_in.astype(jnp.float32) + mixed
    stream_out = summed.astype(jnp.bfloat16)
    scale_stream = jnp.sqrt(jnp.mean(summed * summed, axis=-1, keepdims=True) + 1e-05)
    normed_stream = (summed / scale_stream * norm_gain).astype(jnp.bfloat16)
    in_block = w_qkv.shape[0]
    all_rows = lax.all_gather(normed_stream, ("win", "wout"), axis=0, tiled=True)
    columns = lax.dynamic_slice_in_dim(all_rows, lax.axis_index("win") * in_block, in_block, 1)
    projected = lax.psum_scatter(
        jnp.dot(columns, w_qkv, preferred_element_type=jnp.float32).astype(jnp.bfloat16),
        "win",
        scatter_dimension=0,
        tiled=True,
    )
    return (projected, stream_out, final_states, conv_edges)


def solution(mesh):
    return jax.shard_map(
        body,
        mesh=mesh,
        in_specs=(
            P("seq", None, ("win", "wout")),
            P(None, None, ("win", "wout")),
            P(("win", "wout"), "seq"),
            P(),
            P(),
            P(("win", "wout"), None),
            P(("seq", "win", "wout"), None),
            P(),
            P("win", "wout"),
        ),
        out_specs=(
            P(("seq", "win"), "wout"),
            P(("seq", "win", "wout"), None),
            P(None, ("win", "wout"), None, None),
            P(None, None, None, ("win", "wout")),
        ),
        check_vma=False,
    )
```

profile of v0, /device:TPU:16, one launch (start us, length us, event | category | flops | bytes accessed | tf_op | source)
XLA Modules:
  0.0 699.0 jit_solution(7639928728784033836)
XLA Ops:
  8.9 3.5 collective-permute-start.1
  45.6 40.7 %custom-call.3 = f32[4,2,1,64,64]{3,4,2,1,0:T(8,128)} custom-call(f32[4,2,1,64,64]{4,3,2,1,0:T(8,128)} %fusion.23), custom_call_target="InvertDiagBlocksLowerTriangular" | custom-call | tf_op jit(solution)/shard_map/triangular_solve | solution.py:85
  98.1 9.9 %while.37 = (s32[]{:T(128)}, f32[2,128,128]{2,1,0:T(8,128)S(1)}, f32[2,128,128]{2,1,0:T(8,128)S(1)}, f32[4,2,128,128]{3,2,1,0:T(8,128)}, f32[4,2,128,128]{3,2,1,0:T(8,128)}, /*index=5*/s32[]{:T(128)}, s32[]{:T(128)}) while((s32[]{:T(128)}, f32[2,128,128]{2,1,0:T(8,128)S(1)}, f32[2,128,128]{2,1,0:T(8,128)S(1)}, ...), condition=%wide.region_6.7_spmd.clone, body=%wide.region_5.6_spmd.clone.sunk | while | flops 100728832 | bytes 1443426 | solution.py:116
  108.1 306.8 %while.35 = (s32[]{:T(128)}, f32[2,128,128]{2,1,0:T(8,128)S(1)}, f32[2,128,128]{2,1,0:T(8,128)S(1)}, f32[2,128,128]{2,1,0:T(8,128)S(1)}, s32[]{:T(128)}) while((s32[]{:T(128)}, f32[2,128,128]{2,1,0:T(8,128)S(1)}, f32[2,128,128]{2,1,0:T(8,128)S(1)}, f32[2,128,128]{2,1,0:T(8,128)S(1)}, s32[]{:T(128)}) %tuple.81), condition=%wide.region_8.9_spmd, body=%wide.region_7.8_spmd.sunk | while | flops 50364416 | bytes 1048677 | solution.py:124
  109.0 3.4 collective-permute-start
  116.2 4.2 collective-permute-start
  124.2 4.2 collective-permute-start
  132.2 4.2 collective-permute-start
  140.1 4.2 collective-permute-start
  148.1 6.0 collective-permute-start
  157.8 6.3 collective-permute-start
  167.9 6.5 collective-permute-start
  174.4 3.9 collective-permute-done
  179.2 6.9 collective-permute-start
  186.1 3.4 collective-permute-done
  190.5 6.1 collective-permute-start
  200.3 5.9 collective-permute-start
  210.0 6.4 collective-permute-start
  220.1 6.4 collective-permute-start
  230.3 6.3 collective-permute-start
  240.4 6.3 collective-permute-start
  250.5 6.3 collective-permute-start
  256.8 3.5 collective-permute-done
  261.3 6.7 collective-permute-start
  268.0 3.7 collective-permute-done
  272.6 6.7 collective-permute-start
  283.0 6.0 collective-permute-start
  292.8 6.4 collective-permute-start
  302.9 6.4 collective-permute-start
  313.1 6.3 collective-permute-start
  323.2 6.3 collective-permute-start
  333.3 6.3 collective-permute-start
  339.6 3.1 collective-permute-done
  343.7 6.7 collective-permute-start
  350.4 4.0 collective-permute-done
  355.3 6.4 collective-permute-start
  361.7 3.0 collective-permute-done
  365.6 6.2 collective-permute-start
  375.6 6.2 collective-permute-start
  385.5 6.4 collective-permute-start
  395.7 6.3 collective-permute-start
  405.8 6.3 collective-permute-start
  414.9 7.7 %while.36 = (s32[]{:T(128)}, f32[2,128,128]{2,1,0:T(8,128)S(1)}, f32[4,2,128,128]{3,2,1,0:T(8,128)}, f32[4,2,128,128]{3,2,1,0:T(8,128)}, f32[4,2,128,128]{3,2,1,0:T(8,128)}, /*index=5*/s32[]{:T(128)}) while((s32[]{:T(128)}, f32[2,128,128]{2,1,0:T(8,128)S(1)}, f32[4,2,128,128]{3,2,1,0:T(8,128)}, f32[4,2,128,128]{3,2,1,0:T(8,128)}, ...), condition=%wide.region_10.11_spmd, body=%wide.region_9.10_spmd.sunk | while | flops 50364416 | bytes 1049681 | solution.py:132
  431.1 79.2 %reduce-scatter.3.cloned.1.call-done = bf16[32,2048]{1,0:T(8,128)(2,1)} async-done(((bf16[256,2048]{1,0:T(8,128)(2,1)}), bf16[32,2048]{1,0:T(8,128)(2,1)}) %reduce-scatter.3.cloned.1.call-update) | async-done | bytes 131088 | tf_op jit(solution)/shard_map/reduce_scatter | solution.py:169
  518.5 3.2 fusion.16
  521.8 19.7 %all-gather.2.cloned.1.call-done = bf16[256,2048]{1,0:T(8,128)(2,1)} async-done(((bf16[32,2048]{1,0:T(8,128)(2,1)}), bf16[256,2048]{1,0:T(8,128)(2,1)}) %all-gather.2.cloned.1.call-update) | async-done | bytes 1048592 | tf_op jit(solution)/shard_map/all_gather | solution.py:180
  541.6 3.1 convolution_convert_fusion
  546.9 143.2 %psum.15 = bf16[4,3,3,256]{3,0,2,1:T(4,128)(2,1)} all-reduce(bf16[4,3,3,256]{3,0,2,1:T(4,128)(2,1)} %convolution_convert_fusion.2), channel_id=1, replica_groups=mesh['seq'=32,'win'=4,'wout'=2] {'seq'}, use_global_device_ids=true, to_apply=%region_18.19 | all-reduce | flops 9216 | bytes 36864 | tf_op jit(solution)/shard_map/psum | solution.py:160
  (195 shorter events, 179.8 us)
Async XLA Ops:
  8.0 533.6 %copy-start = (bf16[512,3072]{1,0:T(8,128)(2,1)S(1)}, bf16[512,3072]{1,0:T(8,128)(2,1)}, u32[]{:S(2)}) copy-start(bf16[512,3072]{1,0:T(8,128)(2,1)} %param.23) | copy-start | bytes 9437188
  8.0 502.3 %reduce-scatter.3.cloned.1.call-start = ((), (), s32[]{:S(2)}) async-start(), calls=%async_computation.2 | async-start | bytes 1179648 | tf_op jit(solution)/shard_map/reduce_scatter | solution.py:169
  8.9 12.8 %collective-permute-start.1 = (bf16[3,3,256]{2,0,1:T(4,128)(2,1)S(1)}, bf16[3,3,256]{2,0,1:T(4,128)(2,1)S(1)}, u32[]{:S(2)}, u32[]{:S(2)}) collective-permute-start(bf16[3,3,256]{2,0,1:T(4,128)(2,1)S(1)} %slice.63), channel_id=1, source_target_pairs={{0,8},{8,16},{16,24},{24,32},{32,40},{40,48},{48,56},{56,64},{64,7... | collective-permute-start | bytes 13832 | tf_op jit(solution)/shard_map/ppermute | solution.py:15
  12.5 4.0 copy-start.8
  13.3 3.9 copy-start.12
  43.4 52.3 %copy-start.1 = (f32[4,64,2,128]{3,1,2,0:T(8,128)}, f32[4,64,2,128]{3,1,2,0:T(8,128)S(1)}, u32[]{:S(2)}) copy-start(f32[4,64,2,128]{3,1,2,0:T(8,128)S(1)} %get-tuple-element.164) | copy-start | bytes 786436
  86.3 9.3 %copy-start.5 = (f32[128,128]{1,0:T(8,128)S(1)}, f32[128,128]{1,0:T(8,128)}, u32[]{:S(2)}) copy-start(f32[128,128]{1,0:T(8,128)} %fusion.63) | copy-start | bytes 196612
  88.1 10.0 %copy-start.3 = (f32[4,2,64,256]{3,2,1,0:T(8,128)}, f32[4,2,64,256]{3,2,1,0:T(8,128)S(1)}, u32[]{:S(2)}) copy-start(f32[4,2,64,256]{3,2,1,0:T(8,128)S(1)} %fusion.28) | copy-start | bytes 1572868
  109.0 6.2 collective-permute-start
  116.2 7.1 %collective-permute-start = (f32[2,128,128]{2,1,0:T(8,128)}, f32[2,128,128]{2,1,0:T(8,128)S(1)}, u32[]{:S(2)}, u32[]{:S(2)}) collective-permute-start(f32[2,128,128]{2,1,0:T(8,128)} %convolution_add_fusion.8), channel_id=1, source_target_pairs={{0,8},{8,16},{16,24},{24,32},{32,40},{40,48},{48,56},{56,64},{64,7... | collective-permute-start | bytes 393224 | tf_op jit(solution)/shard_map/while/body/eval_jaxpr/ppermute | solution.py:15
  124.2 7.1 %collective-permute-start = (f32[2,128,128]{2,1,0:T(8,128)}, f32[2,128,128]{2,1,0:T(8,128)S(1)}, u32[]{:S(2)}, u32[]{:S(2)}) collective-permute-start(f32[2,128,128]{2,1,0:T(8,128)} %convolution_add_fusion.8), channel_id=1, source_target_pairs={{0,8},{8,16},{16,24},{24,32},{32,40},{40,48},{48,56},{56,64},{64,7... | collective-permute-start | bytes 393224 | tf_op jit(solution)/shard_map/while/body/eval_jaxpr/ppermute | solution.py:15
  132.2 7.1 %collective-permute-start = (f32[2,128,128]{2,1,0:T(8,128)}, f32[2,128,128]{2,1,0:T(8,128)S(1)}, u32[]{:S(2)}, u32[]{:S(2)}) collective-permute-start(f32[2,128,128]{2,1,0:T(8,128)} %convolution_add_fusion.8), channel_id=1, source_target_pairs={{0,8},{8,16},{16,24},{24,32},{32,40},{40,48},{48,56},{56,64},{64,7... | collective-permute-start | bytes 393224 | tf_op jit(solution)/shard_map/while/body/eval_jaxpr/ppermute | solution.py:15
  140.1 7.1 %collective-permute-start = (f32[2,128,128]{2,1,0:T(8,128)}, f32[2,128,128]{2,1,0:T(8,128)S(1)}, u32[]{:S(2)}, u32[]{:S(2)}) collective-permute-start(f32[2,128,128]{2,1,0:T(8,128)} %convolution_add_fusion.8), channel_id=1, source_target_pairs={{0,8},{8,16},{16,24},{24,32},{32,40},{40,48},{48,56},{56,64},{64,7... | collective-permute-start | bytes 393224 | tf_op jit(solution)/shard_map/while/body/eval_jaxpr/ppermute | solution.py:15
  148.1 8.8 %collective-permute-start = (f32[2,128,128]{2,1,0:T(8,128)}, f32[2,128,128]{2,1,0:T(8,128)S(1)}, u32[]{:S(2)}, u32[]{:S(2)}) collective-permute-start(f32[2,128,128]{2,1,0:T(8,128)} %convolution_add_fusion.8), channel_id=1, source_target_pairs={{0,8},{8,16},{16,24},{24,32},{32,40},{40,48},{48,56},{56,64},{64,7... | collective-permute-start | bytes 393224 | tf_op jit(solution)/shard_map/while/body/eval_jaxpr/ppermute | solution.py:15
  157.8 9.2 %collective-permute-start = (f32[2,128,128]{2,1,0:T(8,128)}, f32[2,128,128]{2,1,0:T(8,128)S(1)}, u32[]{:S(2)}, u32[]{:S(2)}) collective-permute-start(f32[2,128,128]{2,1,0:T(8,128)} %convolution_add_fusion.8), channel_id=1, source_target_pairs={{0,8},{8,16},{16,24},{24,32},{32,40},{40,48},{48,56},{56,64},{64,7... | collective-permute-start | bytes 393224 | tf_op jit(solution)/shard_map/while/body/eval_jaxpr/ppermute | solution.py:15
  167.9 10.3 %collective-permute-start = (f32[2,128,128]{2,1,0:T(8,128)}, f32[2,128,128]{2,1,0:T(8,128)S(1)}, u32[]{:S(2)}, u32[]{:S(2)}) collective-permute-start(f32[2,128,128]{2,1,0:T(8,128)} %convolution_add_fusion.8), channel_id=1, source_target_pairs={{0,8},{8,16},{16,24},{24,32},{32,40},{40,48},{48,56},{56,64},{64,7... | collective-permute-start | bytes 393224 | tf_op jit(solution)/shard_map/while/body/eval_jaxpr/ppermute | solution.py:15
  179.2 10.4 %collective-permute-start = (f32[2,128,128]{2,1,0:T(8,128)}, f32[2,128,128]{2,1,0:T(8,128)S(1)}, u32[]{:S(2)}, u32[]{:S(2)}) collective-permute-start(f32[2,128,128]{2,1,0:T(8,128)} %convolution_add_fusion.8), channel_id=1, source_target_pairs={{0,8},{8,16},{16,24},{24,32},{32,40},{40,48},{48,56},{56,64},{64,7... | collective-permute-start | bytes 393224 | tf_op jit(solution)/shard_map/while/body/eval_jaxpr/ppermute | solution.py:15
  190.5 8.9 %collective-permute-start = (f32[2,128,128]{2,1,0:T(8,128)}, f32[2,128,128]{2,1,0:T(8,128)S(1)}, u32[]{:S(2)}, u32[]{:S(2)}) collective-permute-start(f32[2,128,128]{2,1,0:T(8,128)} %convolution_add_fusion.8), channel_id=1, source_target_pairs={{0,8},{8,16},{16,24},{24,32},{32,40},{40,48},{48,56},{56,64},{64,7... | collective-permute-start | bytes 393224 | tf_op jit(solution)/shard_map/while/body/eval_jaxpr/ppermute | solution.py:15
  200.3 8.7 %collective-permute-start = (f32[2,128,128]{2,1,0:T(8,128)}, f32[2,128,128]{2,1,0:T(8,128)S(1)}, u32[]{:S(2)}, u32[]{:S(2)}) collective-permute-start(f32[2,128,128]{2,1,0:T(8,128)} %convolution_add_fusion.8), channel_id=1, source_target_pairs={{0,8},{8,16},{16,24},{24,32},{32,40},{40,48},{48,56},{56,64},{64,7... | collective-permute-start | bytes 393224 | tf_op jit(solution)/shard_map/while/body/eval_jaxpr/ppermute | solution.py:15
  210.0 9.2 %collective-permute-start = (f32[2,128,128]{2,1,0:T(8,128)}, f32[2,128,128]{2,1,0:T(8,128)S(1)}, u32[]{:S(2)}, u32[]{:S(2)}) collective-permute-start(f32[2,128,128]{2,1,0:T(8,128)} %convolution_add_fusion.8), channel_id=1, source_target_pairs={{0,8},{8,16},{16,24},{24,32},{32,40},{40,48},{48,56},{56,64},{64,7... | collective-permute-start | bytes 393224 | tf_op jit(solution)/shard_map/while/body/eval_jaxpr/ppermute | solution.py:15
  220.1 9.2 %collective-permute-start = (f32[2,128,128]{2,1,0:T(8,128)}, f32[2,128,128]{2,1,0:T(8,128)S(1)}, u32[]{:S(2)}, u32[]{:S(2)}) collective-permute-start(f32[2,128,128]{2,1,0:T(8,128)} %convolution_add_fusion.8), channel_id=1, source_target_pairs={{0,8},{8,16},{16,24},{24,32},{32,40},{40,48},{48,56},{56,64},{64,7... | collective-permute-start | bytes 393224 | tf_op jit(solution)/shard_map/while/body/eval_jaxpr/ppermute | solution.py:15
  230.3 9.2 %collective-permute-start = (f32[2,128,128]{2,1,0:T(8,128)}, f32[2,128,128]{2,1,0:T(8,128)S(1)}, u32[]{:S(2)}, u32[]{:S(2)}) collective-permute-start(f32[2,128,128]{2,1,0:T(8,128)} %convolution_add_fusion.8), channel_id=1, source_target_pairs={{0,8},{8,16},{16,24},{24,32},{32,40},{40,48},{48,56},{56,64},{64,7... | collective-permute-start | bytes 393224 | tf_op jit(solution)/shard_map/while/body/eval_jaxpr/ppermute | solution.py:15
  240.4 9.2 %collective-permute-start = (f32[2,128,128]{2,1,0:T(8,128)}, f32[2,128,128]{2,1,0:T(8,128)S(1)}, u32[]{:S(2)}, u32[]{:S(2)}) collective-permute-start(f32[2,128,128]{2,1,0:T(8,128)} %convolution_add_fusion.8), channel_id=1, source_target_pairs={{0,8},{8,16},{16,24},{24,32},{32,40},{40,48},{48,56},{56,64},{64,7... | collective-permute-start | bytes 393224 | tf_op jit(solution)/shard_map/while/body/eval_jaxpr/ppermute | solution.py:15
  250.5 9.9 %collective-permute-start = (f32[2,128,128]{2,1,0:T(8,128)}, f32[2,128,128]{2,1,0:T(8,128)S(1)}, u32[]{:S(2)}, u32[]{:S(2)}) collective-permute-start(f32[2,128,128]{2,1,0:T(8,128)} %convolution_add_fusion.8), channel_id=1, source_target_pairs={{0,8},{8,16},{16,24},{24,32},{32,40},{40,48},{48,56},{56,64},{64,7... | collective-permute-start | bytes 393224 | tf_op jit(solution)/shard_map/while/body/eval_jaxpr/ppermute | solution.py:15
  261.3 10.4 %collective-permute-start = (f32[2,128,128]{2,1,0:T(8,128)}, f32[2,128,128]{2,1,0:T(8,128)S(1)}, u32[]{:S(2)}, u32[]{:S(2)}) collective-permute-start(f32[2,128,128]{2,1,0:T(8,128)} %convolution_add_fusion.8), channel_id=1, source_target_pairs={{0,8},{8,16},{16,24},{24,32},{32,40},{40,48},{48,56},{56,64},{64,7... | collective-permute-start | bytes 393224 | tf_op jit(solution)/shard_map/while/body/eval_jaxpr/ppermute | solution.py:15
  272.6 9.5 %collective-permute-start = (f32[2,128,128]{2,1,0:T(8,128)}, f32[2,128,128]{2,1,0:T(8,128)S(1)}, u32[]{:S(2)}, u32[]{:S(2)}) collective-permute-start(f32[2,128,128]{2,1,0:T(8,128)} %convolution_add_fusion.8), channel_id=1, source_target_pairs={{0,8},{8,16},{16,24},{24,32},{32,40},{40,48},{48,56},{56,64},{64,7... | collective-permute-start | bytes 393224 | tf_op jit(solution)/shard_map/while/body/eval_jaxpr/ppermute | solution.py:15
  283.0 8.8 %collective-permute-start = (f32[2,128,128]{2,1,0:T(8,128)}, f32[2,128,128]{2,1,0:T(8,128)S(1)}, u32[]{:S(2)}, u32[]{:S(2)}) collective-permute-start(f32[2,128,128]{2,1,0:T(8,128)} %convolution_add_fusion.8), channel_id=1, source_target_pairs={{0,8},{8,16},{16,24},{24,32},{32,40},{40,48},{48,56},{56,64},{64,7... | collective-permute-start | bytes 393224 | tf_op jit(solution)/shard_map/while/body/eval_jaxpr/ppermute | solution.py:15
  292.8 9.2 %collective-permute-start = (f32[2,128,128]{2,1,0:T(8,128)}, f32[2,128,128]{2,1,0:T(8,128)S(1)}, u32[]{:S(2)}, u32[]{:S(2)}) collective-permute-start(f32[2,128,128]{2,1,0:T(8,128)} %convolution_add_fusion.8), channel_id=1, source_target_pairs={{0,8},{8,16},{16,24},{24,32},{32,40},{40,48},{48,56},{56,64},{64,7... | collective-permute-start | bytes 393224 | tf_op jit(solution)/shard_map/while/body/eval_jaxpr/ppermute | solution.py:15
  302.9 9.2 %collective-permute-start = (f32[2,128,128]{2,1,0:T(8,128)}, f32[2,128,128]{2,1,0:T(8,128)S(1)}, u32[]{:S(2)}, u32[]{:S(2)}) collective-permute-start(f32[2,128,128]{2,1,0:T(8,128)} %convolution_add_fusion.8), channel_id=1, source_target_pairs={{0,8},{8,16},{16,24},{24,32},{32,40},{40,48},{48,56},{56,64},{64,7... | collective-permute-start | bytes 393224 | tf_op jit(solution)/shard_map/while/body/eval_jaxpr/ppermute | solution.py:15
  313.1 9.2 %collective-permute-start = (f32[2,128,128]{2,1,0:T(8,128)}, f32[2,128,128]{2,1,0:T(8,128)S(1)}, u32[]{:S(2)}, u32[]{:S(2)}) collective-permute-start(f32[2,128,128]{2,1,0:T(8,128)} %convolution_add_fusion.8), channel_id=1, source_target_pairs={{0,8},{8,16},{16,24},{24,32},{32,40},{40,48},{48,56},{56,64},{64,7... | collective-permute-start | bytes 393224 | tf_op jit(solution)/shard_map/while/body/eval_jaxpr/ppermute | solution.py:15
  323.2 9.2 %collective-permute-start = (f32[2,128,128]{2,1,0:T(8,128)}, f32[2,128,128]{2,1,0:T(8,128)S(1)}, u32[]{:S(2)}, u32[]{:S(2)}) collective-permute-start(f32[2,128,128]{2,1,0:T(8,128)} %convolution_add_fusion.8), channel_id=1, source_target_pairs={{0,8},{8,16},{16,24},{24,32},{32,40},{40,48},{48,56},{56,64},{64,7... | collective-permute-start | bytes 393224 | tf_op jit(solution)/shard_map/while/body/eval_jaxpr/ppermute | solution.py:15
  333.3 9.5 %collective-permute-start = (f32[2,128,128]{2,1,0:T(8,128)}, f32[2,128,128]{2,1,0:T(8,128)S(1)}, u32[]{:S(2)}, u32[]{:S(2)}) collective-permute-start(f32[2,128,128]{2,1,0:T(8,128)} %convolution_add_fusion.8), channel_id=1, source_target_pairs={{0,8},{8,16},{16,24},{24,32},{32,40},{40,48},{48,56},{56,64},{64,7... | collective-permute-start | bytes 393224 | tf_op jit(solution)/shard_map/while/body/eval_jaxpr/ppermute | solution.py:15
  343.7 10.7 %collective-permute-start = (f32[2,128,128]{2,1,0:T(8,128)}, f32[2,128,128]{2,1,0:T(8,128)S(1)}, u32[]{:S(2)}, u32[]{:S(2)}) collective-permute-start(f32[2,128,128]{2,1,0:T(8,128)} %convolution_add_fusion.8), channel_id=1, source_target_pairs={{0,8},{8,16},{16,24},{24,32},{32,40},{40,48},{48,56},{56,64},{64,7... | collective-permute-start | bytes 393224 | tf_op jit(solution)/shard_map/while/body/eval_jaxpr/ppermute | solution.py:15
  355.3 9.4 %collective-permute-start = (f32[2,128,128]{2,1,0:T(8,128)}, f32[2,128,128]{2,1,0:T(8,128)S(1)}, u32[]{:S(2)}, u32[]{:S(2)}) collective-permute-start(f32[2,128,128]{2,1,0:T(8,128)} %convolution_add_fusion.8), channel_id=1, source_target_pairs={{0,8},{8,16},{16,24},{24,32},{32,40},{40,48},{48,56},{56,64},{64,7... | collective-permute-start | bytes 393224 | tf_op jit(solution)/shard_map/while/body/eval_jaxpr/ppermute | solution.py:15
  365.6 9.1 %collective-permute-start = (f32[2,128,128]{2,1,0:T(8,128)}, f32[2,128,128]{2,1,0:T(8,128)S(1)}, u32[]{:S(2)}, u32[]{:S(2)}) collective-permute-start(f32[2,128,128]{2,1,0:T(8,128)} %convolution_add_fusion.8), channel_id=1, source_target_pairs={{0,8},{8,16},{16,24},{24,32},{32,40},{40,48},{48,56},{56,64},{64,7... | collective-permute-start | bytes 393224 | tf_op jit(solution)/shard_map/while/body/eval_jaxpr/ppermute | solution.py:15
  375.6 9.0 %collective-permute-start = (f32[2,128,128]{2,1,0:T(8,128)}, f32[2,128,128]{2,1,0:T(8,128)S(1)}, u32[]{:S(2)}, u32[]{:S(2)}) collective-permute-start(f32[2,128,128]{2,1,0:T(8,128)} %convolution_add_fusion.8), channel_id=1, source_target_pairs={{0,8},{8,16},{16,24},{24,32},{32,40},{40,48},{48,56},{56,64},{64,7... | collective-permute-start | bytes 393224 | tf_op jit(solution)/shard_map/while/body/eval_jaxpr/ppermute | solution.py:15
  385.5 9.2 %collective-permute-start = (f32[2,128,128]{2,1,0:T(8,128)}, f32[2,128,128]{2,1,0:T(8,128)S(1)}, u32[]{:S(2)}, u32[]{:S(2)}) collective-permute-start(f32[2,128,128]{2,1,0:T(8,128)} %convolution_add_fusion.8), channel_id=1, source_target_pairs={{0,8},{8,16},{16,24},{24,32},{32,40},{40,48},{48,56},{56,64},{64,7... | collective-permute-start | bytes 393224 | tf_op jit(solution)/shard_map/while/body/eval_jaxpr/ppermute | solution.py:15
  395.7 9.2 %collective-permute-start = (f32[2,128,128]{2,1,0:T(8,128)}, f32[2,128,128]{2,1,0:T(8,128)S(1)}, u32[]{:S(2)}, u32[]{:S(2)}) collective-permute-start(f32[2,128,128]{2,1,0:T(8,128)} %convolution_add_fusion.8), channel_id=1, source_target_pairs={{0,8},{8,16},{16,24},{24,32},{32,40},{40,48},{48,56},{56,64},{64,7... | collective-permute-start | bytes 393224 | tf_op jit(solution)/shard_map/while/body/eval_jaxpr/ppermute | solution.py:15
  405.8 9.2 %collective-permute-start = (f32[2,128,128]{2,1,0:T(8,128)}, f32[2,128,128]{2,1,0:T(8,128)S(1)}, u32[]{:S(2)}, u32[]{:S(2)}) collective-permute-start(f32[2,128,128]{2,1,0:T(8,128)} %convolution_add_fusion.8), channel_id=1, source_target_pairs={{0,8},{8,16},{16,24},{24,32},{32,40},{40,48},{48,56},{56,64},{64,7... | collective-permute-start | bytes 393224 | tf_op jit(solution)/shard_map/while/body/eval_jaxpr/ppermute | solution.py:15
  414.9 7.7 %copy-start.4 = (f32[4,2,64,128]{3,2,1,0:T(8,128)S(1)}, f32[4,2,64,128]{3,2,1,0:T(8,128)}, u32[]{:S(2)}) copy-start(f32[4,2,64,128]{3,2,1,0:T(8,128)} %fusion.56) | copy-start | bytes 786436
  422.7 87.6 %copy-start.6 = (bf16[32,2048]{1,0:T(8,128)(2,1)S(1)}, bf16[32,2048]{1,0:T(8,128)(2,1)}, u32[]{:S(2)}) copy-start(bf16[32,2048]{1,0:T(8,128)(2,1)} %param.21) | copy-start | bytes 393220
  427.1 89.4 %copy-start.2 = (f32[4,64,2,128]{3,1,2,0:T(8,128)S(1)}, f32[4,64,2,128]{3,1,2,0:T(8,128)}, u32[]{:S(2)}) copy-start(f32[4,64,2,128]{3,1,2,0:T(8,128)} %copy-done.1) | copy-start | bytes 786436
  431.0 110.5 %all-gather.2.cloned.1.call-start = ((), (), s32[]{:S(2)}) async-start(), calls=%async_computation.3 | async-start | bytes 1179648 | tf_op jit(solution)/shard_map/all_gather | solution.py:180
  513.1 177.0 %all-reduce.2.cloned.1.call-start = ((), (), s32[]{:S(2)}) async-start(), calls=%async_computation.5 | async-start | bytes 524288 | tf_op jit(solution)/shard_map/psum | solution.py:159
  521.8 24.2 %copy-start.7 = (bf16[256,3,256]{2,0,1:T(8,128)(2,1)S(1)}, bf16[256,3,256]{2,0,1:T(8,128)(2,1)}, u32[]{:S(2)}) copy-start(bf16[256,3,256]{2,0,1:T(8,128)(2,1)} %param.15) | copy-start | bytes 1179652
  521.8 24.2 %copy-start.9 = (s32[259]{0:T(512)S(1)}, s32[259]{0:T(512)}, u32[]{:S(2)}) copy-start(s32[259]{0:T(512)} %copy-done.8) | copy-start | bytes 3112
  521.8 24.2 %copy-start.11 = (bf16[3,3,256]{2,0,1:T(4,128)(2,1)S(1)}, bf16[3,3,256]{2,0,1:T(4,128)(2,1)}, u32[]{:S(2)}) copy-start(bf16[3,3,256]{2,0,1:T(4,128)(2,1)} %copy-done.10) | copy-start | bytes 13828
  521.8 170.1 %reduce-scatter.5.cloned.1.call-start = ((), (), s32[]{:S(2)}) async-start(), calls=%async_computation.4 | async-start | bytes 1966080 | tf_op jit(solution)/shard_map/reduce_scatter | solution.py:182
  (1 other events, 0.6 us)
Sparse Core Ops, SparseCore 0:
  431.2 79.0 reduce-scatter.2
  513.2 28.3 all-gather.1
  544.9 27.9 reduce-scatter.4
Sparse Core Ops, SparseCore 1:
  521.9 147.6 all-reduce.1
where the time goes:
time: 701 us; the launch traced here: 699 us
  waiting for transfers between devices  191 us (27%)
  starting transfers between devices  190 us (27%)
  blocking collectives  143 us (20%)
  matrix products  73.4 us (10%)
  other arithmetic  63.6 us (9%)
  local copies, waits for them, and re-layouts  22.1 us (3%)
  between operations  15.5 us (2%)
    ppermute x32, starting transfers between devices, from_behind(): lax.ppermute(value, axis, [(source, source + steps) for source in range(l...  189 us
    psum x1, blocking collectives, body(): lax.psum(edge_vals.astype(jnp.bfloat16), 'seq').astype(jnp.float32)  143 us
    ppermute x32, waiting for transfers between devices, from_behind(): lax.ppermute(value, axis, [(source, source + steps) for source in range(l...  92 us
    reduce_scatter x1, waiting for transfers between devices, body(): lax.psum_scatter(jnp.dot(normed_heads, w_out, preferred_element_type=jnp....  79.2 us
    dot_general x52, matrix products, outer_product(): return jnp.einsum(form, left, right, precision=lax.Precision.HIGHEST)  63 us
    another operation x4, other arithmetic, body(): lax.linalg.triangular_solve(system, targets, left_side=True, lower=True,...  42 us
    all_gather x1, waiting for transfers between devices, body(): lax.all_gather(normed_stream, ('win', 'wout'), axis=0, tiled=True)  19.7 us
  transfers between devices with their start and end apart: 36, of which 33 were waited for; matrix products, arithmetic and copies ran while one was open for 4% of the time, Pallas kernels for 0%

commit v1 on v0

--- a/solution.py
+++ b/solution.py
@@ -177,7 +177,12 @@
     scale_stream = jnp.sqrt(jnp.mean(summed * summed, axis=-1, keepdims=True) + 1e-05)
     normed_stream = (summed / scale_stream * norm_gain).astype(jnp.bfloat16)
     in_block = w_qkv.shape[0]
-    all_rows = lax.all_gather(normed_stream, ("win", "wout"), axis=0, tiled=True)
+    all_rows = jnp.concatenate(
+        lax.all_to_all(
+            jnp.stack([normed_stream] * lax.axis_size(("win", "wout"))), ("win", "wout"), 0, 0
+        ),
+        axis=0,
+    )
     columns = lax.dynamic_slice_in_dim(all_rows, lax.axis_index("win") * in_block, in_block, 1)
     projected = lax.psum_scatter(
         jnp.dot(columns, w_qkv, preferred_element_type=jnp.float32).astype(jnp.bfloat16),

time: 701 us -> 697 us (level)
  waiting for transfers between devices: 191 us -> 176 us
  starting transfers between devices: 190 us -> 199 us
    all_gather x1 -> x0, waiting for transfers between devices: 19.7 us -> none  [body(): lax.all_gather(normed_stream, ('win', 'wout'), axis=0, tiled=True)]
    all_to_all x0 -> x1, starting transfers between devices: none -> 9.56 us  [body(): lax.all_to_all(jnp.stack([normed_stream] * lax.axis_size(('win', 'wout'))...]
where the time goes in v1:
time: 697 us; the launch traced here: 693 us
  starting transfers between devices  199 us (29%)
  waiting for transfers between devices  176 us (25%)
  blocking collectives  143 us (21%)
  matrix products  73.4 us (11%)
  other arithmetic  63.6 us (9%)
  local copies, waits for them, and re-layouts  21.7 us (3%)
  between operations  15.8 us (2%)
    ppermute x32, starting transfers between devices, from_behind(): lax.ppermute(value, axis, [(source, source + steps) for source in range(l...  189 us
    psum x1, blocking collectives, body(): lax.psum(edge_vals.astype(jnp.bfloat16), 'seq').astype(jnp.float32)  143 us
    ppermute x32, waiting for transfers between devices, from_behind(): lax.ppermute(value, axis, [(source, source + steps) for source in range(l...  92 us
    reduce_scatter x1, waiting for transfers between devices, body(): lax.psum_scatter(jnp.dot(normed_heads, w_out, preferred_element_type=jnp....  78 us
    dot_general x52, matrix products, outer_product(): return jnp.einsum(form, left, right, precision=lax.Precision.HIGHEST)  62.9 us
    another operation x4, other arithmetic, body(): lax.linalg.triangular_solve(system, targets, left_side=True, lower=True,...  42 us
  transfers between devices with their start and end apart: 36, of which 33 were waited for; matrix products, arithmetic and copies ran while one was open for 4% of the time, Pallas kernels for 0%

profile of v1, /device:TPU:16, one launch (start us, length us, event | category | flops | bytes accessed | tf_op | source)
XLA Modules:
  0.0 692.8 jit_solution(943529609787550159)
XLA Ops:
  8.9 3.5 collective-permute-start.1
  45.6 40.7 %custom-call.3 = f32[4,2,1,64,64]{3,4,2,1,0:T(8,128)} custom-call(f32[4,2,1,64,64]{4,3,2,1,0:T(8,128)} %fusion.23), custom_call_target="InvertDiagBlocksLowerTriangular" | custom-call | tf_op jit(solution)/shard_map/triangular_solve | solution.py:85
  98.1 9.9 %while.37 = (s32[]{:T(128)}, f32[2,128,128]{2,1,0:T(8,128)S(1)}, f32[2,128,128]{2,1,0:T(8,128)S(1)}, f32[4,2,128,128]{3,2,1,0:T(8,128)}, f32[4,2,128,128]{3,2,1,0:T(8,128)}, /*index=5*/s32[]{:T(128)}, s32[]{:T(128)}) while((s32[]{:T(128)}, f32[2,128,128]{2,1,0:T(8,128)S(1)}, f32[2,128,128]{2,1,0:T(8,128)S(1)}, ...), condition=%wide.region_6.7_spmd.clone, body=%wide.region_5.6_spmd.clone.sunk | while | flops 100728832 | bytes 1443426 | solution.py:116
  108.0 306.8 %while.35 = (s32[]{:T(128)}, f32[2,128,128]{2,1,0:T(8,128)S(1)}, f32[2,128,128]{2,1,0:T(8,128)S(1)}, f32[2,128,128]{2,1,0:T(8,128)S(1)}, s32[]{:T(128)}) while((s32[]{:T(128)}, f32[2,128,128]{2,1,0:T(8,128)S(1)}, f32[2,128,128]{2,1,0:T(8,128)S(1)}, f32[2,128,128]{2,1,0:T(8,128)S(1)}, s32[]{:T(128)}) %tuple.81), condition=%wide.region_8.9_spmd, body=%wide.region_7.8_spmd.sunk | while | flops 50364416 | bytes 1048677 | solution.py:124
  109.0 3.4 collective-permute-start
  116.1 4.2 collective-permute-start
  124.1 4.2 collective-permute-start
  132.1 4.2 collective-permute-start
  140.1 4.2 collective-permute-start
  148.1 6.0 collective-permute-start
  157.8 6.3 collective-permute-start
  167.9 6.5 collective-permute-start
  174.3 3.9 collective-permute-done
  179.1 6.9 %collective-permute-start = (f32[2,128,128]{2,1,0:T(8,128)}, f32[2,128,128]{2,1,0:T(8,128)S(1)}, u32[]{:S(2)}, u32[]{:S(2)}) collective-permute-start(f32[2,128,128]{2,1,0:T(8,128)} %convolution_add_fusion.8), channel_id=1, source_target_pairs={{0,8},{8,16},{16,24},{24,32},{32,40},{40,48},{48,56},{56,64},{64,7... | collective-permute-start | bytes 393224 | tf_op jit(solution)/shard_map/while/body/eval_jaxpr/ppermute | solution.py:15
  186.1 3.4 collective-permute-done
  190.4 6.1 collective-permute-start
  200.3 5.9 collective-permute-start
  209.9 6.4 collective-permute-start
  220.1 6.4 collective-permute-start
  230.2 6.3 collective-permute-start
  240.3 6.3 collective-permute-start
  250.4 6.3 collective-permute-start
  256.8 3.5 collective-permute-done
  261.2 6.7 collective-permute-start
  267.9 3.7 collective-permute-done
  272.5 6.7 collective-permute-start
  283.0 6.0 collective-permute-start
  292.7 6.4 collective-permute-start
  302.9 6.4 collective-permute-start
  313.0 6.3 collective-permute-start
  323.1 6.3 collective-permute-start
  333.2 6.3 collective-permute-start
  339.6 3.1 collective-permute-done
  343.6 6.7 collective-permute-start
  350.3 4.0 collective-permute-done
  355.3 6.4 collective-permute-start
  365.5 6.2 collective-permute-start
  375.5 6.2 collective-permute-start
  385.5 6.4 collective-permute-start
  395.6 6.3 collective-permute-start
  405.7 6.3 collective-permute-start
  414.9 7.7 %while.36 = (s32[]{:T(128)}, f32[2,128,128]{2,1,0:T(8,128)S(1)}, f32[4,2,128,128]{3,2,1,0:T(8,128)}, f32[4,2,128,128]{3,2,1,0:T(8,128)}, f32[4,2,128,128]{3,2,1,0:T(8,128)}, /*index=5*/s32[]{:T(128)}) while((s32[]{:T(128)}, f32[2,128,128]{2,1,0:T(8,128)S(1)}, f32[4,2,128,128]{3,2,1,0:T(8,128)}, f32[4,2,128,128]{3,2,1,0:T(8,128)}, ...), condition=%wide.region_10.11_spmd, body=%wide.region_9.10_spmd.sunk | while | flops 50364416 | bytes 1049681 | solution.py:132
  430.6 78.0 %reduce-scatter.3.cloned.1.call-done = bf16[32,2048]{1,0:T(8,128)(2,1)} async-done(((bf16[256,2048]{1,0:T(8,128)(2,1)}), bf16[32,2048]{1,0:T(8,128)(2,1)}) %reduce-scatter.3.cloned.1.call-update) | async-done | bytes 131088 | tf_op jit(solution)/shard_map/reduce_scatter | solution.py:169
  512.5 9.6 %all-to-all-start = ((bf16[8,32,2048]{2,1,0:T(8,128)(2,1)}), bf16[8,32,2048]{2,1,0:T(8,128)(2,1)}, u32[]{:S(2)}, u32[]{:S(2)}) async-start(bf16[8,32,2048]{2,1,0:T(8,128)(2,1)} %stack.2), calls=%async_computation.1 | async-start | bytes 2097152 | tf_op jit(solution)/shard_map/all_to_all | solution.py:181
  526.1 3.2 fusion.16
  529.4 5.5 all-to-all-done
  534.9 3.1 convolution_convert_fusion
  540.3 143.2 %psum.15 = bf16[4,3,3,256]{3,0,2,1:T(4,128)(2,1)} all-reduce(bf16[4,3,3,256]{3,0,2,1:T(4,128)(2,1)} %convolution_convert_fusion.2), channel_id=1, replica_groups=mesh['seq'=32,'win'=4,'wout'=2] {'seq'}, use_global_device_ids=true, to_apply=%region_18.19 | all-reduce | flops 9216 | bytes 36864 | tf_op jit(solution)/shard_map/psum | solution.py:160
  (197 shorter events, 182.1 us)
Async XLA Ops:
  8.0 526.9 %copy-start = (bf16[512,3072]{1,0:T(8,128)(2,1)S(1)}, bf16[512,3072]{1,0:T(8,128)(2,1)}, u32[]{:S(2)}) copy-start(bf16[512,3072]{1,0:T(8,128)(2,1)} %param.23) | copy-start | bytes 9437188
  8.0 500.7 %reduce-scatter.3.cloned.1.call-start = ((), (), s32[]{:S(2)}) async-start(), calls=%async_computation.3 | async-start | bytes 1179648 | tf_op jit(solution)/shard_map/reduce_scatter | solution.py:169
  8.9 12.7 %collective-permute-start.1 = (bf16[3,3,256]{2,0,1:T(4,128)(2,1)S(1)}, bf16[3,3,256]{2,0,1:T(4,128)(2,1)S(1)}, u32[]{:S(2)}, u32[]{:S(2)}) collective-permute-start(bf16[3,3,256]{2,0,1:T(4,128)(2,1)S(1)} %slice.63), channel_id=1, source_target_pairs={{0,8},{8,16},{16,24},{24,32},{32,40},{40,48},{48,56},{56,64},{64,7... | collective-permute-start | bytes 13832 | tf_op jit(solution)/shard_map/ppermute | solution.py:15
  12.5 4.0 copy-start.8
  43.4 52.2 %copy-start.1 = (f32[4,64,2,128]{3,1,2,0:T(8,128)}, f32[4,64,2,128]{3,1,2,0:T(8,128)S(1)}, u32[]{:S(2)}) copy-start(f32[4,64,2,128]{3,1,2,0:T(8,128)S(1)} %get-tuple-element.164) | copy-start | bytes 786436
  86.3 9.3 %copy-start.5 = (f32[128,128]{1,0:T(8,128)S(1)}, f32[128,128]{1,0:T(8,128)}, u32[]{:S(2)}) copy-start(f32[128,128]{1,0:T(8,128)} %fusion.63) | copy-start | bytes 196612
  88.1 10.0 %copy-start.3 = (f32[4,2,64,256]{3,2,1,0:T(8,128)}, f32[4,2,64,256]{3,2,1,0:T(8,128)S(1)}, u32[]{:S(2)}) copy-start(f32[4,2,64,256]{3,2,1,0:T(8,128)S(1)} %fusion.28) | copy-start | bytes 1572868
  109.0 6.2 collective-permute-start
  116.1 7.1 %collective-permute-start = (f32[2,128,128]{2,1,0:T(8,128)}, f32[2,128,128]{2,1,0:T(8,128)S(1)}, u32[]{:S(2)}, u32[]{:S(2)}) collective-permute-start(f32[2,128,128]{2,1,0:T(8,128)} %convolution_add_fusion.8), channel_id=1, source_target_pairs={{0,8},{8,16},{16,24},{24,32},{32,40},{40,48},{48,56},{56,64},{64,7... | collective-permute-start | bytes 393224 | tf_op jit(solution)/shard_map/while/body/eval_jaxpr/ppermute | solution.py:15
  124.1 7.1 %collective-permute-start = (f32[2,128,128]{2,1,0:T(8,128)}, f32[2,128,128]{2,1,0:T(8,128)S(1)}, u32[]{:S(2)}, u32[]{:S(2)}) collective-permute-start(f32[2,128,128]{2,1,0:T(8,128)} %convolution_add_fusion.8), channel_id=1, source_target_pairs={{0,8},{8,16},{16,24},{24,32},{32,40},{40,48},{48,56},{56,64},{64,7... | collective-permute-start | bytes 393224 | tf_op jit(solution)/shard_map/while/body/eval_jaxpr/ppermute | solution.py:15
  132.1 7.1 %collective-permute-start = (f32[2,128,128]{2,1,0:T(8,128)}, f32[2,128,128]{2,1,0:T(8,128)S(1)}, u32[]{:S(2)}, u32[]{:S(2)}) collective-permute-start(f32[2,128,128]{2,1,0:T(8,128)} %convolution_add_fusion.8), channel_id=1, source_target_pairs={{0,8},{8,16},{16,24},{24,32},{32,40},{40,48},{48,56},{56,64},{64,7... | collective-permute-start | bytes 393224 | tf_op jit(solution)/shard_map/while/body/eval_jaxpr/ppermute | solution.py:15
  140.1 7.1 %collective-permute-start = (f32[2,128,128]{2,1,0:T(8,128)}, f32[2,128,128]{2,1,0:T(8,128)S(1)}, u32[]{:S(2)}, u32[]{:S(2)}) collective-permute-start(f32[2,128,128]{2,1,0:T(8,128)} %convolution_add_fusion.8), channel_id=1, source_target_pairs={{0,8},{8,16},{16,24},{24,32},{32,40},{40,48},{48,56},{56,64},{64,7... | collective-permute-start | bytes 393224 | tf_op jit(solution)/shard_map/while/body/eval_jaxpr/ppermute | solution.py:15
  148.1 8.8 %collective-permute-start = (f32[2,128,128]{2,1,0:T(8,128)}, f32[2,128,128]{2,1,0:T(8,128)S(1)}, u32[]{:S(2)}, u32[]{:S(2)}) collective-permute-start(f32[2,128,128]{2,1,0:T(8,128)} %convolution_add_fusion.8), channel_id=1, source_target_pairs={{0,8},{8,16},{16,24},{24,32},{32,40},{40,48},{48,56},{56,64},{64,7... | collective-permute-start | bytes 393224 | tf_op jit(solution)/shard_map/while/body/eval_jaxpr/ppermute | solution.py:15
  157.8 9.2 %collective-permute-start = (f32[2,128,128]{2,1,0:T(8,128)}, f32[2,128,128]{2,1,0:T(8,128)S(1)}, u32[]{:S(2)}, u32[]{:S(2)}) collective-permute-start(f32[2,128,128]{2,1,0:T(8,128)} %convolution_add_fusion.8), channel_id=1, source_target_pairs={{0,8},{8,16},{16,24},{24,32},{32,40},{40,48},{48,56},{56,64},{64,7... | collective-permute-start | bytes 393224 | tf_op jit(solution)/shard_map/while/body/eval_jaxpr/ppermute | solution.py:15
  167.9 10.3 %collective-permute-start = (f32[2,128,128]{2,1,0:T(8,128)}, f32[2,128,128]{2,1,0:T(8,128)S(1)}, u32[]{:S(2)}, u32[]{:S(2)}) collective-permute-start(f32[2,128,128]{2,1,0:T(8,128)} %convolution_add_fusion.8), channel_id=1, source_target_pairs={{0,8},{8,16},{16,24},{24,32},{32,40},{40,48},{48,56},{56,64},{64,7... | collective-permute-start | bytes 393224 | tf_op jit(solution)/shard_map/while/body/eval_jaxpr/ppermute | solution.py:15
  179.1 10.4 %collective-permute-start = (f32[2,128,128]{2,1,0:T(8,128)}, f32[2,128,128]{2,1,0:T(8,128)S(1)}, u32[]{:S(2)}, u32[]{:S(2)}) collective-permute-start(f32[2,128,128]{2,1,0:T(8,128)} %convolution_add_fusion.8), channel_id=1, source_target_pairs={{0,8},{8,16},{16,24},{24,32},{32,40},{40,48},{48,56},{56,64},{64,7... | collective-permute-start | bytes 393224 | tf_op jit(solution)/shard_map/while/body/eval_jaxpr/ppermute | solution.py:15
  190.4 9.0 %collective-permute-start = (f32[2,128,128]{2,1,0:T(8,128)}, f32[2,128,128]{2,1,0:T(8,128)S(1)}, u32[]{:S(2)}, u32[]{:S(2)}) collective-permute-start(f32[2,128,128]{2,1,0:T(8,128)} %convolution_add_fusion.8), channel_id=1, source_target_pairs={{0,8},{8,16},{16,24},{24,32},{32,40},{40,48},{48,56},{56,64},{64,7... | collective-permute-start | bytes 393224 | tf_op jit(solution)/shard_map/while/body/eval_jaxpr/ppermute | solution.py:15
  200.3 8.7 %collective-permute-start = (f32[2,128,128]{2,1,0:T(8,128)}, f32[2,128,128]{2,1,0:T(8,128)S(1)}, u32[]{:S(2)}, u32[]{:S(2)}) collective-permute-start(f32[2,128,128]{2,1,0:T(8,128)} %convolution_add_fusion.8), channel_id=1, source_target_pairs={{0,8},{8,16},{16,24},{24,32},{32,40},{40,48},{48,56},{56,64},{64,7... | collective-permute-start | bytes 393224 | tf_op jit(solution)/shard_map/while/body/eval_jaxpr/ppermute | solution.py:15
  209.9 9.2 %collective-permute-start = (f32[2,128,128]{2,1,0:T(8,128)}, f32[2,128,128]{2,1,0:T(8,128)S(1)}, u32[]{:S(2)}, u32[]{:S(2)}) collective-permute-start(f32[2,128,128]{2,1,0:T(8,128)} %convolution_add_fusion.8), channel_id=1, source_target_pairs={{0,8},{8,16},{16,24},{24,32},{32,40},{40,48},{48,56},{56,64},{64,7... | collective-permute-start | bytes 393224 | tf_op jit(solution)/shard_map/while/body/eval_jaxpr/ppermute | solution.py:15
  220.1 9.2 %collective-permute-start = (f32[2,128,128]{2,1,0:T(8,128)}, f32[2,128,128]{2,1,0:T(8,128)S(1)}, u32[]{:S(2)}, u32[]{:S(2)}) collective-permute-start(f32[2,128,128]{2,1,0:T(8,128)} %convolution_add_fusion.8), channel_id=1, source_target_pairs={{0,8},{8,16},{16,24},{24,32},{32,40},{40,48},{48,56},{56,64},{64,7... | collective-permute-start | bytes 393224 | tf_op jit(solution)/shard_map/while/body/eval_jaxpr/ppermute | solution.py:15
  230.2 9.2 %collective-permute-start = (f32[2,128,128]{2,1,0:T(8,128)}, f32[2,128,128]{2,1,0:T(8,128)S(1)}, u32[]{:S(2)}, u32[]{:S(2)}) collective-permute-start(f32[2,128,128]{2,1,0:T(8,128)} %convolution_add_fusion.8), channel_id=1, source_target_pairs={{0,8},{8,16},{16,24},{24,32},{32,40},{40,48},{48,56},{56,64},{64,7... | collective-permute-start | bytes 393224 | tf_op jit(solution)/shard_map/while/body/eval_jaxpr/ppermute | solution.py:15
  240.3 9.2 %collective-permute-start = (f32[2,128,128]{2,1,0:T(8,128)}, f32[2,128,128]{2,1,0:T(8,128)S(1)}, u32[]{:S(2)}, u32[]{:S(2)}) collective-permute-start(f32[2,128,128]{2,1,0:T(8,128)} %convolution_add_fusion.8), channel_id=1, source_target_pairs={{0,8},{8,16},{16,24},{24,32},{32,40},{40,48},{48,56},{56,64},{64,7... | collective-permute-start | bytes 393224 | tf_op jit(solution)/shard_map/while/body/eval_jaxpr/ppermute | solution.py:15
  250.4 9.9 %collective-permute-start = (f32[2,128,128]{2,1,0:T(8,128)}, f32[2,128,128]{2,1,0:T(8,128)S(1)}, u32[]{:S(2)}, u32[]{:S(2)}) collective-permute-start(f32[2,128,128]{2,1,0:T(8,128)} %convolution_add_fusion.8), channel_id=1, source_target_pairs={{0,8},{8,16},{16,24},{24,32},{32,40},{40,48},{48,56},{56,64},{64,7... | collective-permute-start | bytes 393224 | tf_op jit(solution)/shard_map/while/body/eval_jaxpr/ppermute | solution.py:15
  261.2 10.4 %collective-permute-start = (f32[2,128,128]{2,1,0:T(8,128)}, f32[2,128,128]{2,1,0:T(8,128)S(1)}, u32[]{:S(2)}, u32[]{:S(2)}) collective-permute-start(f32[2,128,128]{2,1,0:T(8,128)} %convolution_add_fusion.8), channel_id=1, source_target_pairs={{0,8},{8,16},{16,24},{24,32},{32,40},{40,48},{48,56},{56,64},{64,7... | collective-permute-start | bytes 393224 | tf_op jit(solution)/shard_map/while/body/eval_jaxpr/ppermute | solution.py:15
  272.5 9.5 %collective-permute-start = (f32[2,128,128]{2,1,0:T(8,128)}, f32[2,128,128]{2,1,0:T(8,128)S(1)}, u32[]{:S(2)}, u32[]{:S(2)}) collective-permute-start(f32[2,128,128]{2,1,0:T(8,128)} %convolution_add_fusion.8), channel_id=1, source_target_pairs={{0,8},{8,16},{16,24},{24,32},{32,40},{40,48},{48,56},{56,64},{64,7... | collective-permute-start | bytes 393224 | tf_op jit(solution)/shard_map/while/body/eval_jaxpr/ppermute | solution.py:15
  283.0 8.8 %collective-permute-start = (f32[2,128,128]{2,1,0:T(8,128)}, f32[2,128,128]{2,1,0:T(8,128)S(1)}, u32[]{:S(2)}, u32[]{:S(2)}) collective-permute-start(f32[2,128,128]{2,1,0:T(8,128)} %convolution_add_fusion.8), channel_id=1, source_target_pairs={{0,8},{8,16},{16,24},{24,32},{32,40},{40,48},{48,56},{56,64},{64,7... | collective-permute-start | bytes 393224 | tf_op jit(solution)/shard_map/while/body/eval_jaxpr/ppermute | solution.py:15
  292.7 9.2 %collective-permute-start = (f32[2,128,128]{2,1,0:T(8,128)}, f32[2,128,128]{2,1,0:T(8,128)S(1)}, u32[]{:S(2)}, u32[]{:S(2)}) collective-permute-start(f32[2,128,128]{2,1,0:T(8,128)} %convolution_add_fusion.8), channel_id=1, source_target_pairs={{0,8},{8,16},{16,24},{24,32},{32,40},{40,48},{48,56},{56,64},{64,7... | collective-permute-start | bytes 393224 | tf_op jit(solution)/shard_map/while/body/eval_jaxpr/ppermute | solution.py:15
  302.9 9.2 %collective-permute-start = (f32[2,128,128]{2,1,0:T(8,128)}, f32[2,128,128]{2,1,0:T(8,128)S(1)}, u32[]{:S(2)}, u32[]{:S(2)}) collective-permute-start(f32[2,128,128]{2,1,0:T(8,128)} %convolution_add_fusion.8), channel_id=1, source_target_pairs={{0,8},{8,16},{16,24},{24,32},{32,40},{40,48},{48,56},{56,64},{64,7... | collective-permute-start | bytes 393224 | tf_op jit(solution)/shard_map/while/body/eval_jaxpr/ppermute | solution.py:15
  313.0 9.2 %collective-permute-start = (f32[2,128,128]{2,1,0:T(8,128)}, f32[2,128,128]{2,1,0:T(8,128)S(1)}, u32[]{:S(2)}, u32[]{:S(2)}) collective-permute-start(f32[2,128,128]{2,1,0:T(8,128)} %convolution_add_fusion.8), channel_id=1, source_target_pairs={{0,8},{8,16},{16,24},{24,32},{32,40},{40,48},{48,56},{56,64},{64,7... | collective-permute-start | bytes 393224 | tf_op jit(solution)/shard_map/while/body/eval_jaxpr/ppermute | solution.py:15
  323.1 9.2 %collective-permute-start = (f32[2,128,128]{2,1,0:T(8,128)}, f32[2,128,128]{2,1,0:T(8,128)S(1)}, u32[]{:S(2)}, u32[]{:S(2)}) collective-permute-start(f32[2,128,128]{2,1,0:T(8,128)} %convolution_add_fusion.8), channel_id=1, source_target_pairs={{0,8},{8,16},{16,24},{24,32},{32,40},{40,48},{48,56},{56,64},{64,7... | collective-permute-start | bytes 393224 | tf_op jit(solution)/shard_map/while/body/eval_jaxpr/ppermute | solution.py:15
  333.2 9.5 %collective-permute-start = (f32[2,128,128]{2,1,0:T(8,128)}, f32[2,128,128]{2,1,0:T(8,128)S(1)}, u32[]{:S(2)}, u32[]{:S(2)}) collective-permute-start(f32[2,128,128]{2,1,0:T(8,128)} %convolution_add_fusion.8), channel_id=1, source_target_pairs={{0,8},{8,16},{16,24},{24,32},{32,40},{40,48},{48,56},{56,64},{64,7... | collective-permute-start | bytes 393224 | tf_op jit(solution)/shard_map/while/body/eval_jaxpr/ppermute | solution.py:15
  343.6 10.7 %collective-permute-start = (f32[2,128,128]{2,1,0:T(8,128)}, f32[2,128,128]{2,1,0:T(8,128)S(1)}, u32[]{:S(2)}, u32[]{:S(2)}) collective-permute-start(f32[2,128,128]{2,1,0:T(8,128)} %convolution_add_fusion.8), channel_id=1, source_target_pairs={{0,8},{8,16},{16,24},{24,32},{32,40},{40,48},{48,56},{56,64},{64,7... | collective-permute-start | bytes 393224 | tf_op jit(solution)/shard_map/while/body/eval_jaxpr/ppermute | solution.py:15
  355.3 9.4 %collective-permute-start = (f32[2,128,128]{2,1,0:T(8,128)}, f32[2,128,128]{2,1,0:T(8,128)S(1)}, u32[]{:S(2)}, u32[]{:S(2)}) collective-permute-start(f32[2,128,128]{2,1,0:T(8,128)} %convolution_add_fusion.8), channel_id=1, source_target_pairs={{0,8},{8,16},{16,24},{24,32},{32,40},{40,48},{48,56},{56,64},{64,7... | collective-permute-start | bytes 393224 | tf_op jit(solution)/shard_map/while/body/eval_jaxpr/ppermute | solution.py:15
  365.5 9.1 %collective-permute-start = (f32[2,128,128]{2,1,0:T(8,128)}, f32[2,128,128]{2,1,0:T(8,128)S(1)}, u32[]{:S(2)}, u32[]{:S(2)}) collective-permute-start(f32[2,128,128]{2,1,0:T(8,128)} %convolution_add_fusion.8), channel_id=1, source_target_pairs={{0,8},{8,16},{16,24},{24,32},{32,40},{40,48},{48,56},{56,64},{64,7... | collective-permute-start | bytes 393224 | tf_op jit(solution)/shard_map/while/body/eval_jaxpr/ppermute | solution.py:15
  375.5 9.0 %collective-permute-start = (f32[2,128,128]{2,1,0:T(8,128)}, f32[2,128,128]{2,1,0:T(8,128)S(1)}, u32[]{:S(2)}, u32[]{:S(2)}) collective-permute-start(f32[2,128,128]{2,1,0:T(8,128)} %convolution_add_fusion.8), channel_id=1, source_target_pairs={{0,8},{8,16},{16,24},{24,32},{32,40},{40,48},{48,56},{56,64},{64,7... | collective-permute-start | bytes 393224 | tf_op jit(solution)/shard_map/while/body/eval_jaxpr/ppermute | solution.py:15
  385.5 9.2 %collective-permute-start = (f32[2,128,128]{2,1,0:T(8,128)}, f32[2,128,128]{2,1,0:T(8,128)S(1)}, u32[]{:S(2)}, u32[]{:S(2)}) collective-permute-start(f32[2,128,128]{2,1,0:T(8,128)} %convolution_add_fusion.8), channel_id=1, source_target_pairs={{0,8},{8,16},{16,24},{24,32},{32,40},{40,48},{48,56},{56,64},{64,7... | collective-permute-start | bytes 393224 | tf_op jit(solution)/shard_map/while/body/eval_jaxpr/ppermute | solution.py:15
  395.6 9.2 %collective-permute-start = (f32[2,128,128]{2,1,0:T(8,128)}, f32[2,128,128]{2,1,0:T(8,128)S(1)}, u32[]{:S(2)}, u32[]{:S(2)}) collective-permute-start(f32[2,128,128]{2,1,0:T(8,128)} %convolution_add_fusion.8), channel_id=1, source_target_pairs={{0,8},{8,16},{16,24},{24,32},{32,40},{40,48},{48,56},{56,64},{64,7... | collective-permute-start | bytes 393224 | tf_op jit(solution)/shard_map/while/body/eval_jaxpr/ppermute | solution.py:15
  405.7 9.2 %collective-permute-start = (f32[2,128,128]{2,1,0:T(8,128)}, f32[2,128,128]{2,1,0:T(8,128)S(1)}, u32[]{:S(2)}, u32[]{:S(2)}) collective-permute-start(f32[2,128,128]{2,1,0:T(8,128)} %convolution_add_fusion.8), channel_id=1, source_target_pairs={{0,8},{8,16},{16,24},{24,32},{32,40},{40,48},{48,56},{56,64},{64,7... | collective-permute-start | bytes 393224 | tf_op jit(solution)/shard_map/while/body/eval_jaxpr/ppermute | solution.py:15
  414.9 7.8 %copy-start.4 = (f32[4,2,64,128]{3,2,1,0:T(8,128)S(1)}, f32[4,2,64,128]{3,2,1,0:T(8,128)}, u32[]{:S(2)}) copy-start(f32[4,2,64,128]{3,2,1,0:T(8,128)} %fusion.56) | copy-start | bytes 786436
  422.6 86.1 %copy-start.6 = (bf16[32,2048]{1,0:T(8,128)(2,1)S(1)}, bf16[32,2048]{1,0:T(8,128)(2,1)}, u32[]{:S(2)}) copy-start(bf16[32,2048]{1,0:T(8,128)(2,1)} %param.21) | copy-start | bytes 393220
  429.4 94.8 %copy-start.2 = (f32[4,64,2,128]{3,1,2,0:T(8,128)S(1)}, f32[4,64,2,128]{3,1,2,0:T(8,128)}, u32[]{:S(2)}) copy-start(f32[4,64,2,128]{3,1,2,0:T(8,128)} %copy-done.1) | copy-start | bytes 786436
  511.4 10.7 %copy-start.13 = (s32[4]{0:T(128)S(1)}, s32[4]{0:T(128)}, u32[]{:S(2)}) copy-start(s32[4]{0:T(128)} %get-tuple-element.184) | copy-start | bytes 52
  512.5 22.4 %all-to-all-start = ((bf16[8,32,2048]{2,1,0:T(8,128)(2,1)}), bf16[8,32,2048]{2,1,0:T(8,128)(2,1)}, u32[]{:S(2)}, u32[]{:S(2)}) async-start(bf16[8,32,2048]{2,1,0:T(8,128)(2,1)} %stack.2), calls=%async_computation.1 | async-start | bytes 2097152 | tf_op jit(solution)/shard_map/all_to_all | solution.py:181
  522.0 161.6 %all-reduce.2.cloned.1.call-start = ((), (), s32[]{:S(2)}) async-start(), calls=%async_computation.5 | async-start | bytes 524288 | tf_op jit(solution)/shard_map/psum | solution.py:159
  529.4 156.0 %reduce-scatter.5.cloned.1.call-start = ((), (), s32[]{:S(2)}) async-start(), calls=%async_computation.4 | async-start | bytes 1966080 | tf_op jit(solution)/shard_map/reduce_scatter | solution.py:187
  534.9 4.5 copy-start.7
  534.9 4.5 copy-start.9
  534.9 4.6 copy-start.11
  (2 other events, 4.5 us)
Sparse Core Ops, SparseCore 0:
  429.5 79.1 reduce-scatter.2
  538.2 28.8 reduce-scatter.4
Sparse Core Ops, SparseCore 1:
  529.5 145.2 all-reduce.1
